TPU v7x, 128 devices: a whole 4x4x4 slice. The times are simulated.
128 devices in a mesh: seq: 32 (over z_hi, y, x), head: 4 (over z_lo, core).
Axes of the slice: x: 4, y: 4, z: 4 (z_hi: 2, z_lo: 2; z = z_hi * 2 + z_lo), core: 2. Of those that a mesh axis runs over, the one named last changes fastest.
Arguments:
- x_in: bfloat16 [16384, 4096], P('seq', 'head'), may hold values from -6 to 6
- z_in: bfloat16 [16384, 4096], P('seq', 'head'), may hold values from -6 to 6
- b_in: bfloat16 [16384, 512], P('seq', 'head'), may hold values from -0.5 to 0.5
- c_in: bfloat16 [16384, 512], P('seq', 'head'), may hold values from -0.5 to 0.5
- dt_raw: float32 [64, 16384], P('head', 'seq')
- dt_bias: float32 [64], P('head'), may hold values from -5 to -4
- a_log: float32 [64], P('head')
- d_skip: float32 [64], P('head'), may hold values from 0.1 to 1.9
- gain: float32 [4096], P('head'), may hold values from 0.5 to 1.5
- resets: int32 [64, 128], P('head', 'seq'), may hold values 0 or 1
- out_weight: bfloat16 [4096, 4096], P('seq', 'head'), may hold values from -0.09375 to 0.09375
- cotangent: bfloat16 [16384, 4096], P('seq', 'head'), may hold values from -6 to 6
Outputs:
- d_x: bfloat16 [16384, 4096], P('seq', 'head')
- d_z: bfloat16 [16384, 4096], P('seq', 'head')
- d_b: bfloat16 [16384, 512], P('seq', 'head')
- d_c: bfloat16 [16384, 512], P('seq', 'head')
- raw_timestep_gradient: float32 [64, 16384], P('head', 'seq')
- d_out_weight: float32 [4096, 4096], P('seq', 'head')
All inputs are finite; a program needn't handle non-finite values. No bound on the sum of `resets` on one device may be relied on, other than what follows from the above.
Results may differ from a plain program's by a relative error of at most 0.0075.
Values may be sent and summed in bfloat16 or wider, within the bound.
A program may use at most 256 MiB of HBM per device.

v0:
```python
from functools import partial
import jax
import jax.numpy as jnp
from jax import lax
from jax.sharding import PartitionSpec as P

HEADDIM = 64
STATE = 128
BLOCK = 128
highest = lax.Precision.HIGHEST


def prefix(value, axis, join, neutral, backward):
    count, mine = (lax.axis_size(axis), lax.axis_index(axis))
    pieces = jax.tree.map(lambda part: lax.all_gather(part, axis), value)
    if backward:
        pieces = jax.tree.map(lambda part: part[::-1], pieces)
        mine = count - 1 - mine
    so_far = jax.tree.map(
        lambda part, zero: jnp.full_like(part, 0) + jnp.asarray(zero, part.dtype), value, neutral
    )

    def step(position, so_far):
        longer = join(so_far, jax.tree.map(lambda part: part[position], pieces))
        return jax.tree.map(lambda new, old: jnp.where(position < mine, new, old), longer, so_far)

    return lax.fori_loop(0, count - 1, step, so_far)


def block_step(state, inputs, per_group, skip_gain):
    x_block, b_block, c_block, rate_block, step_block, keep_block = inputs
    running = jnp.cumsum(rate_block, axis=1)
    positions = rate_block.shape[1]
    lower = jnp.arange(positions)[:, None] >= jnp.arange(positions)[None, :]
    spread = jnp.where(lower[None], running[:, :, None] - running[:, None, :], 0.0)
    decays = jnp.exp(spread) * lower[None].astype(jnp.float32)
    scores = jnp.einsum("tgn,sgn->gts", c_block, b_block, precision=highest)
    scores = jnp.repeat(scores, per_group, axis=0)
    mixing = scores * decays * step_block[:, None, :]
    within = jnp.einsum("hts,shp->thp", mixing, x_block, precision=highest)
    c_heads = jnp.repeat(c_block, per_group, axis=1)
    b_heads = jnp.repeat(b_block, per_group, axis=1)
    carried = state * keep_block[:, None, None]
    incoming = (
        jnp.einsum("thn,hpn->thp", c_heads, carried, precision=highest)
        * jnp.exp(running).T[:, :, None]
    )
    output = within + incoming + skip_gain[None, :, None] * x_block
    weighted = (jnp.exp(running[:, -1:] - running) * step_block).T
    fresh = jnp.einsum("sh,shp,shn->hpn", weighted, x_block, b_heads, precision=highest)
    return (carried * jnp.exp(running[:, -1])[:, None, None] + fresh, output)


def scan_blocks(inputs, bmatrix, cmatrix, dt_raw, start, dt_bias, a_log, d_skip, keep):
    positions = inputs.shape[0]
    heads = dt_raw.shape[0]
    groups = bmatrix.shape[1] // STATE
    blocks = positions // BLOCK
    step_size = jax.nn.softplus(dt_raw + dt_bias[:, None])
    rate = -step_size * jnp.exp(a_log)[:, None]
    x_blocks = inputs.reshape(blocks, BLOCK, heads, HEADDIM)
    b_blocks = bmatrix.reshape(blocks, BLOCK, groups, STATE)
    c_blocks = cmatrix.reshape(blocks, BLOCK, groups, STATE)
    rate_blocks = rate.reshape(heads, blocks, BLOCK).transpose(1, 0, 2)
    step_blocks = step_size.reshape(heads, blocks, BLOCK).transpose(1, 0, 2)
    stepper = partial(block_step, per_group=heads // groups, skip_gain=d_skip)
    final, outputs = lax.scan(
        stepper, start, (x_blocks, b_blocks, c_blocks, rate_blocks, step_blocks, keep.T)
    )
    return (outputs.reshape(positions, heads * HEADDIM), final)


def gate_norm(mixed, gates, gain, groups):
    gated = mixed * jax.nn.silu(gates)
    count = gated.shape[0]
    grouped = gated.reshape(count, groups, -1)
    factor = lax.rsqrt(jnp.mean(grouped * grouped, axis=2, keepdims=True) + 1e-05)
    return (grouped * factor).reshape(count, -1) * gain


def compose(earlier, later):
    return (earlier[0] * later[0], later[0][:, None, None] * earlier[1] + later[1])


def body(
    x_in, z_in, b_in, c_in, dt_raw, dt_bias, a_log, d_skip, gain, resets, out_weight, cotangent
):
    heads = dt_raw.shape[0]
    groups = b_in.shape[1] // STATE
    per_group = heads // groups
    positions = x_in.shape[0]
    keep = 1.0 - resets.astype(jnp.float32)
    x_wide = x_in.astype(jnp.float32)
    input_matrix_wide = b_in.astype(jnp.float32)
    c_wide = c_in.astype(jnp.float32)
    z_wide = z_in.astype(jnp.float32)
    zero_state = jnp.zeros((heads, HEADDIM, STATE), jnp.float32)
    step_size = jax.nn.softplus(dt_raw + dt_bias[:, None])
    rate = -step_size * jnp.exp(a_log)[:, None]
    running = jnp.cumsum(rate, axis=1)
    suffix_rates = jnp.flip(jnp.cumsum(jnp.flip(rate, axis=1), axis=1), axis=1)
    after_rates = jnp.concatenate([suffix_rates[:, 1:], jnp.zeros((heads, 1), jnp.float32)], axis=1)
    keep_upto = jnp.repeat(jnp.cumprod(keep, axis=1), BLOCK, axis=1)
    keep_suffix = jnp.flip(jnp.cumprod(jnp.flip(keep, axis=1), axis=1), axis=1)
    keep_after = jnp.concatenate([keep_suffix[:, 1:], jnp.ones((heads, 1), jnp.float32)], axis=1)
    keep_after = jnp.repeat(keep_after, BLOCK, axis=1)
    to_end = jnp.exp(after_rates) * keep_after * step_size
    x_heads = x_wide.reshape(positions, groups, per_group, HEADDIM)
    b_groups = input_matrix_wide.reshape(positions, groups, STATE)
    c_groups = c_wide.reshape(positions, groups, STATE)
    end_weights = to_end.T.reshape(positions, groups, per_group)
    local_final = jnp.einsum(
        "tgq,tgqp,tgn->gqpn", end_weights, x_heads, b_groups, precision=highest
    ).reshape(heads, HEADDIM, STATE)
    slab_decay = jnp.exp(running[:, -1]) * jnp.prod(keep, axis=1)
    identity = (jnp.ones((heads,), jnp.float32), zero_state)
    entering = prefix((slab_decay, local_final), "seq", compose, identity, False)[1]

    def mixer(x_value, b_value, c_value, raw_steps, start_state):
        return scan_blocks(
            x_value, b_value, c_value, raw_steps, start_state, dt_bias, a_log, d_skip, keep
        )

    (mixed, leaving), mixer_pull = jax.vjp(
        mixer, x_wide, input_matrix_wide, c_wide, dt_raw, entering
    )

    def norming(mixed_value, z_value):
        return gate_norm(mixed_value, z_value, gain, groups)

    normed, norm_pull = jax.vjp(norming, mixed, z_wide)
    normed_half = normed.astype(jnp.bfloat16)
    gathered = lax.all_gather(cotangent, "head", axis=1, tiled=True)
    columns = gathered
    d_normed = jnp.dot(
        columns,
        lax.all_gather(out_weight, "seq", axis=0, tiled=True),
        preferred_element_type=jnp.float32,
    )
    d_mixed, grad_z = norm_pull(d_normed)
    from_start = (jnp.exp(running) * keep_upto).T.reshape(positions, groups, per_group)
    d_heads = d_mixed.reshape(positions, groups, per_group, HEADDIM)
    start_grad = jnp.einsum(
        "tgq,tgqp,tgn->gqpn", from_start, d_heads, c_groups, precision=highest
    ).reshape(heads, HEADDIM, STATE)
    arriving = prefix((slab_decay, start_grad), "seq", compose, identity, True)[1]
    grad_x, grad_b, grad_c, grad_steps, unused = mixer_pull((d_mixed, arriving))
    columns = gathered
    d_out_weight = lax.psum_scatter(
        jnp.einsum("td,ti->di", columns, normed_half, preferred_element_type=jnp.float32),
        "seq",
        scatter_dimension=0,
        tiled=True,
    )
    return (
        grad_x.astype(jnp.bfloat16),
        grad_z.astype(jnp.bfloat16),
        grad_b.astype(jnp.bfloat16),
        grad_c.astype(jnp.bfloat16),
        grad_steps,
        d_out_weight,
    )


def solution(mesh):
    return jax.shard_map(
        body,
        mesh=mesh,
        in_specs=(
            P("seq", "head"),
            P("seq", "head"),
            P("seq", "head"),
            P("seq", "head"),
            P("head", "seq"),
            P("head"),
            P("head"),
            P("head"),
            P("head"),
            P("head", "seq"),
            P("seq", "head"),
            P("seq", "head"),
        ),
        out_specs=(
            P("seq", "head"),
            P("seq", "head"),
            P("seq", "head"),
            P("seq", "head"),
            P("head", "seq"),
            P("seq", "head"),
        ),
        check_vma=False,
    )
```

profile of v0, /device:TPU:0, one launch (start us, length us, event | category | flops | bytes accessed | tf_op | source)
XLA Modules:
  0.0 738.4 jit_solution(9167421800133413308)
XLA Ops:
  21.2 96.0 %all-gather.2 = f32[32,1,16]{2,1,0:T(1,128)S(1)} all-gather(f32[1,1,16]{2,1,0:T(1,128)S(1)} %fusion.127), channel_id=1, replica_groups=mesh['seq'=32,'head'=4] {'seq'}, dimensions={0}, use_global_device_ids=true | all-gather | bytes 2112 | tf_op jit(solution)/shard_map/all_gather | solution.py:15
  120.9 54.4 %all-gather.12.cloned.1.call-done = f32[512,64,128]{2,1,0:T(8,128)} async-done(((f32[16,64,128]{2,1,0:T(8,128)}), f32[512,64,128]{2,1,0:T(8,128)}) %all-gather.12.cloned.1.call-update) | async-done | bytes 16777232 | tf_op jit(solution)/shard_map/all_gather | solution.py:15
  175.3 37.9 %while.110 = (s32[]{:T(128)}, f32[16,64,128]{2,1,0:T(8,128)S(1)}, s32[]{:T(128)}, f32[32,16]{1,0:T(8,128)S(1)}, f32[32,16,64,128]{3,2,1,0:T(8,128)}) while((s32[]{:T(128)}, f32[16,64,128]{2,1,0:T(8,128)S(1)}, s32[]{:T(128)}, f32[32,16]{1,0:T(8,128)S(1)}, f32[32,16,64,128]{3,2,1,0:T(8,128)}) %tuple.254), condition=%wide.region_8.9_spmd.clone.clone, body=%wide.region_7.8_spmd.clone.sunk.clone | while | flops 524292 | bytes 1573145 | solution.py:27
  216.0 83.1 %while.109 = (s32[]{:T(128)}, f32[16,64,128]{2,1,0:T(8,128)S(1)}, f32[4,128,16,64]{1,3,2,0:T(8,128)}, f32[4,16,128,128]{3,2,1,0:T(8,128)}, f32[4,16,128,128]{3,2...) while((s32[]{:T(128)}, f32[16,64,128]{2,1,0:T(8,128)S(1)}, ...), condition=%wide.region_11.12_spmd.clone.clone.clone, body=%wide.region_9.11_spmd.clone.clone.sunk.clone | while | flops 633511936 | bytes 16000793 | solution.py:67
  225.1 3.7 fusion.254
  245.9 3.7 fusion.254
  266.6 3.7 fusion.254
  281.3 3.2 multiply_dynamic-update-slice_fusion.3
  287.5 3.7 fusion.254
  299.2 4.7 copy.179
  303.9 4.8 reshape.531
  308.8 21.7 %all-gather.10.cloned.1.call-done = bf16[4096,1024]{1,0:T(8,128)(2,1)} async-done(((bf16[128,1024]{1,0:T(8,128)(2,1)}), bf16[4096,1024]{1,0:T(8,128)(2,1)}) %all-gather.10.cloned.1.call-update) | async-done | bytes 8388624 | tf_op jit(solution)/shard_map/all_gather | solution.py:137
  330.4 10.6 %multiply_reduce_fusion.1 = (f32[512]{0:T(512)S(1)}, f32[512]{0:T(512)S(1)}, f32[512,1024]{1,0:T(8,128)S(1)}) fusion(f32[512,1024]{1,0:T(8,128)} %reshape.531, bf16[512,1024]{1,0:T(8,128)(2,1)} %param.21, f32[1024]{0:T(1024)S(1)} %copy-done.15, bf16[512,4096]{1,0:T(8,128)(2,1)} %all-gather.8.cloned.1.call-done, ...), kind=kOutput, calls=%fused_computation.184 | convolution fusion | flops 4300733440 | bytes 17833984 | tf_op jit(solution)/shard_map/dot_general | solution.py:135
  341.0 3.6 fusion.104
  346.6 3.5 fusion.105
  350.1 13.9 %convolution_bitcast_fusion.4 = f32[4096,1024]{0,1:T(8,128)} fusion(bf16[512,4096]{1,0:T(8,128)(2,1)} %all-gather.8.cloned.1.call-done, f32[512]{0:T(512)S(1)} %get-tuple-element.1859, f32[1024]{0:T(1024)S(1)} %copy-done.15, f32[512,1024]{1,0:T(8,128)} %reshape.531, bf16[512,1024]{1,0:T(8,128)(2,1)} %param.21), kind=kOutput, calls=%fused_computation.168 | convolution fusion | flops 4299685888 | bytes 24123392 | tf_op jit(solution)/shard_map/td,ti->di/dot_general | solution.py:150
  368.8 3.1 copy.152
  371.8 132.6 %all-gather.14.cloned.1.call-done = f32[512,64,128]{2,1,0:T(8,128)} async-done(((f32[16,64,128]{2,1,0:T(8,128)}), f32[512,64,128]{2,1,0:T(8,128)}) %all-gather.14.cloned.1.call-update) | async-done | bytes 16777232 | tf_op jit(solution)/shard_map/all_gather | solution.py:15
  504.5 11.8 %rev.19 = f32[32,16,64,128]{3,2,1,0:T(8,128)} reverse(f32[32,16,64,128]{3,2,1,0:T(8,128)} %bitcast.594), dimensions={0} | reverse | bytes 33554432 | tf_op jit(solution)/shard_map/rev | solution.py:17
  516.3 37.7 %while.111 = (s32[]{:T(128)}, f32[16,64,128]{2,1,0:T(8,128)S(1)}, s32[]{:T(128)}, f32[32,16]{1,0:T(8,128)S(1)}, f32[32,16,64,128]{3,2,1,0:T(8,128)}) while((s32[]{:T(128)}, f32[16,64,128]{2,1,0:T(8,128)S(1)}, s32[]{:T(128)}, f32[32,16]{1,0:T(8,128)S(1)}, f32[32,16,64,128]{3,2,1,0:T(8,128)}) %tuple.234), condition=%wide.region_15.16_spmd.clone.clone, body=%wide.region_14.15_spmd.clone.sunk.clone | while | flops 524292 | bytes 1573145 | solution.py:27
  556.7 163.1 %while.108 = (s32[]{:T(128)}, f32[16,64,128]{2,1,0:T(8,128)S(1)}, bf16[4,128,16,64]{1,3,2,0:T(8,128)(2,1)}, bf16[4,128,1,128]{3,1,2,0:T(8,128)(2,1)}, bf16[4,128...) while((s32[]{:T(128)}, f32[16,64,128]{2,1,0:T(8,128)S(1)}, ...), condition=%wide.region_25.26_spmd.clone.clone, body=%wide.region_16.25_spmd.clone.sunk.clone | while | flops 1263466496 | bytes 32037560 | solution.py:67
  559.6 3.3 fusion.236
  567.2 5.0 fusion.238
  585.5 3.1 fusion.237
  600.3 3.3 fusion.236
  608.0 5.0 fusion.238
  626.3 3.1 fusion.237
  641.0 3.3 fusion.236
  648.7 5.0 fusion.238
  681.7 3.3 fusion.236
  689.3 5.0 fusion.238
  707.6 3.1 fusion.237
  (487 shorter events, 300.3 us)
Async XLA Ops:
  7.2 168.2 %all-gather.12.cloned.1.call-start = ((), (), s32[]{:S(2)}) async-start(), calls=%async_computation.4 | async-start | bytes 17301504 | tf_op jit(solution)/shard_map/all_gather | solution.py:15
  7.9 0.9 copy-start.16
  13.3 0.8 copy-start.5
  13.3 0.8 copy-start.13
  13.3 0.9 copy-start.3
  14.2 3.5 copy-start.12
  16.2 292.6 %all-gather.8.cloned.1.call-start = ((), (), s32[]{:S(2)}) async-start(), calls=%async_computation.1 | async-start | bytes 5242880 | tf_op jit(solution)/shard_map/all_gather | solution.py:133
  16.9 313.5 %all-gather.10.cloned.1.call-start = ((), (), s32[]{:S(2)}) async-start(), calls=%async_computation.2 | async-start | bytes 8650752 | tf_op jit(solution)/shard_map/all_gather | solution.py:137
  17.6 486.8 %all-gather.14.cloned.1.call-start = ((), (), s32[]{:S(2)}) async-start(), calls=%async_computation.5 | async-start | bytes 17301504 | tf_op jit(solution)/shard_map/all_gather | solution.py:15
  117.3 1.9 copy-start.4
  299.2 4.8 copy-start.1
  303.9 26.5 %copy-start.15 = (f32[1024]{0:T(1024)S(1)}, f32[1024]{0:T(1024)}, u32[]{:S(2)}) copy-start(f32[1024]{0:T(1024)} %param.28) | copy-start | bytes 12292
  330.4 10.6 %copy-start.2 = (f32[512,1024]{1,0:T(8,128)S(1)}, f32[512,1024]{1,0:T(8,128)}, u32[]{:S(2)}) copy-start(f32[512,1024]{1,0:T(8,128)} %reshape.531) | copy-start | bytes 6291460
  350.1 379.5 %reduce-scatter.2.cloned.1.call-start = ((), (), s32[]{:S(2)}) async-start(), calls=%async_computation.3 | async-start | bytes 17301504 | tf_op jit(solution)/shard_map/reduce_scatter | solution.py:149
  585.5 6.6 copy-start
  590.6 5.8 copy-start.9
  592.1 4.6 copy-start.7
  597.0 0.7 copy-start.8
  626.3 6.5 copy-start
  631.4 5.7 copy-start.9
  632.7 4.6 copy-start.7
  637.7 0.7 copy-start.8
  666.9 6.5 copy-start
  672.0 5.8 copy-start.9
  673.4 4.6 copy-start.7
  707.6 6.6 copy-start
  712.8 5.8 copy-start.9
  714.2 4.6 copy-start.7
  723.5 2.3 copy-start.6
  723.5 2.3 copy-start.11
  723.5 2.3 copy-start.14
  723.5 2.3 copy-start.17
  (6 other events, 4.0 us)
Sparse Core Ops, SparseCore 0:
  16.3 159.0 all-gather.11
  177.0 43.7 all-gather.7
  223.9 106.4 all-gather.9
  350.2 154.2 all-gather.13
  506.7 222.8 reduce-scatter.1
where the time goes:
time: 749 us; the launch traced here: 738 us
  waiting for transfers between devices  213 us (28%)
  other arithmetic  151 us (20%)
  local copies, waits for them, and re-layouts  131 us (17%)
  matrix products  131 us (17%)
  blocking collectives  96 us (13%)
  between operations  14.4 us (2%)
    all_gather x2, waiting for transfers between devices, prefix(): pieces = jax.tree.map(lambda part: lax.all_gather(part, axis), value)  187 us
    all_gather x1, blocking collectives, prefix(): pieces = jax.tree.map(lambda part: lax.all_gather(part, axis), value)  96 us
    select_n x62, other arithmetic, step(): jnp.where(position < mine, new, old)  73.1 us
    dot_general x12, matrix products, block_step(): within = jnp.einsum('hts,shp->thp', mixing, x_block, precision=highest)  47 us
    dynamic_update_slice x24, other arithmetic, scan_blocks(): lax.scan(stepper, start, (x_blocks, b_blocks, c_blocks, rate_blocks, step...  26.9 us
    dynamic_slice x20, local copies, waits for them, and re-layouts, scan_blocks(): lax.scan(stepper, start, (x_blocks, b_blocks, c_blocks, rate_blocks, step...  25.7 us
    dot_general x12, matrix products, block_step(): jnp.einsum('thn,hpn->thp', c_heads, carried, precision=highest)  25.6 us
    dot_general x12, matrix products, block_step(): jnp.einsum('sh,shp,shn->hpn', weighted, x_block, b_heads, precision=highest)  25.3 us
  transfers between devices with their start and end apart: 5, of which 4 were waited for; matrix products, arithmetic and copies ran while one was open for 51% of the time, Pallas kernels for 0%

commit v1 on v0

--- a/solution.py
+++ b/solution.py
@@ -134,7 +134,9 @@
     columns = gathered
     d_normed = jnp.dot(
         columns,
-        lax.all_gather(out_weight, "seq", axis=0, tiled=True),
+        jnp.concatenate(
+            lax.all_to_all(jnp.stack(lax.axis_size("seq") * [out_weight]), "seq", 0, 0), axis=0
+        ),
         preferred_element_type=jnp.float32,
     )
     d_mixed, grad_z = norm_pull(d_normed)

time: 749 us -> 821 us (1.096)
  blocking collectives: 96 us -> 211 us
  waiting for transfers between devices: 213 us -> 155 us
  starting transfers between devices: 0.2 us -> 11.1 us
    all_gather x1, blocking collectives: 96 us -> 211 us  [prefix(): pieces = jax.tree.map(lambda part: lax.all_gather(part, axis), value)]
    all_gather x2, waiting for transfers between devices: 187 us -> 152 us  [prefix(): pieces = jax.tree.map(lambda part: lax.all_gather(part, axis), value)]
    all_gather x1 -> x0, waiting for transfers between devices: 21.7 us -> none  [body(): lax.all_gather(out_weight, 'seq', axis=0, tiled=True)]
    all_to_all x0 -> x1, starting transfers between devices: none -> 11 us  [body(): lax.all_to_all(jnp.stack(lax.axis_size('seq') * [out_weight]), 'seq', 0, 0)]
  transfers between devices with their start and end apart: 5 -> 5, of which waited for: 4 -> 3; matrix products, arithmetic and copies ran while one was open for 51% -> 47% of each run, Pallas kernels for 0% -> 0%
where the time goes in v1:
time: 821 us; the launch traced here: 810 us
  blocking collectives  211 us (26%)
  waiting for transfers between devices  155 us (19%)
  other arithmetic  149 us (18%)
  local copies, waits for them, and re-layouts  135 us (16%)
  matrix products  131 us (16%)
  between operations  14.4 us (2%)
  starting transfers between devices  11.1 us (1%)
    all_gather x1, blocking collectives, prefix(): pieces = jax.tree.map(lambda part: lax.all_gather(part, axis), value)  211 us
    all_gather x2, waiting for transfers between devices, prefix(): pieces = jax.tree.map(lambda part: lax.all_gather(part, axis), value)  152 us
    select_n x62, other arithmetic, step(): jnp.where(position < mine, new, old)  73.1 us
    dot_general x12, matrix products, block_step(): within = jnp.einsum('hts,shp->thp', mixing, x_block, precision=highest)  46.9 us
    dynamic_update_slice x24, other arithmetic, scan_blocks(): lax.scan(stepper, start, (x_blocks, b_blocks, c_blocks, rate_blocks, step...  26.5 us
    dynamic_slice x20, local copies, waits for them, and re-layouts, scan_blocks(): lax.scan(stepper, start, (x_blocks, b_blocks, c_blocks, rate_blocks, step...  25.7 us
    dot_general x12, matrix products, block_step(): jnp.einsum('thn,hpn->thp', c_heads, carried, precision=highest)  25.6 us
    dot_general x12, matrix products, block_step(): jnp.einsum('sh,shp,shn->hpn', weighted, x_block, b_heads, precision=highest)  25.3 us
  transfers between devices with their start and end apart: 5, of which 3 were waited for; matrix products, arithmetic and copies ran while one was open for 47% of the time, Pallas kernels for 0%

profile of v1, /device:TPU:0, one launch (start us, length us, event | category | flops | bytes accessed | tf_op | source)
XLA Modules:
  0.0 809.7 jit_solution(17563684810643973997)
XLA Ops:
  16.2 4.3 stack.2
  20.4 11.0 %all-to-all-start = ((bf16[32,128,1024]{2,1,0:T(8,128)(2,1)}), bf16[32,128,1024]{2,1,0:T(8,128)(2,1)}, u32[]{:S(2)}, u32[]{:S(2)}) async-start(bf16[32,128,1024]{2,1,0:T(8,128)(2,1)} %stack.2), calls=%async_computation | async-start | bytes 16777216 | tf_op jit(solution)/shard_map/all_to_all | solution.py:138
  35.8 211.2 %all-gather.2 = f32[32,1,16]{2,1,0:T(1,128)S(1)} all-gather(f32[1,1,16]{2,1,0:T(1,128)S(1)} %fusion.127), channel_id=1, replica_groups=mesh['seq'=32,'head'=4] {'seq'}, dimensions={0}, use_global_device_ids=true | all-gather | bytes 2112 | tf_op jit(solution)/shard_map/all_gather | solution.py:15
  250.7 19.5 %all-gather.9.cloned.1.call-done = f32[512,64,128]{2,1,0:T(8,128)} async-done(((f32[16,64,128]{2,1,0:T(8,128)}), f32[512,64,128]{2,1,0:T(8,128)}) %all-gather.9.cloned.1.call-update) | async-done | bytes 16777232 | tf_op jit(solution)/shard_map/all_gather | solution.py:15
  270.1 37.9 %while.110 = (s32[]{:T(128)}, f32[16,64,128]{2,1,0:T(8,128)S(1)}, s32[]{:T(128)}, f32[32,16]{1,0:T(8,128)S(1)}, f32[32,16,64,128]{3,2,1,0:T(8,128)}) while((s32[]{:T(128)}, f32[16,64,128]{2,1,0:T(8,128)S(1)}, s32[]{:T(128)}, f32[32,16]{1,0:T(8,128)S(1)}, f32[32,16,64,128]{3,2,1,0:T(8,128)}) %tuple.252), condition=%wide.region_8.9_spmd.clone.clone, body=%wide.region_7.8_spmd.clone.sunk.clone | while | flops 524292 | bytes 1573145 | solution.py:27
  310.8 82.7 %while.109 = (s32[]{:T(128)}, f32[16,64,128]{2,1,0:T(8,128)S(1)}, f32[4,128,16,64]{1,3,2,0:T(8,128)}, f32[4,16,128,128]{3,2,1,0:T(8,128)}, f32[4,16,128,128]{3,2...) while((s32[]{:T(128)}, f32[16,64,128]{2,1,0:T(8,128)S(1)}, ...), condition=%wide.region_11.12_spmd.clone.clone.clone, body=%wide.region_9.11_spmd.clone.clone.sunk.clone | while | flops 633511936 | bytes 16000793 | solution.py:67
  319.9 3.7 fusion.254
  340.6 3.7 fusion.254
  361.3 3.7 fusion.254
  381.8 3.7 fusion.254
  393.5 4.8 copy.179
  398.3 4.9 reshape.537
  403.2 10.6 %multiply_reduce_fusion.1 = (f32[512]{0:T(512)S(1)}, f32[512]{0:T(512)S(1)}, f32[512,1024]{1,0:T(8,128)S(1)}) fusion(f32[512,1024]{1,0:T(8,128)} %reshape.537, bf16[512,1024]{1,0:T(8,128)(2,1)} %param.21, f32[1024]{0:T(1024)S(1)} %copy-done.17, bf16[512,4096]{1,0:T(8,128)(2,1)} %all-gather.7.cloned.1.call-done, bf16[4096,1024]{1,0:T(8,128)(2,1)} %bitcast.6), kind=kOutput, calls=%fused_computation.184 | convolution fusion | flops 4300733440 | bytes 17833984 | tf_op jit(solution)/shard_map/dot_general | solution.py:135
  418.4 3.5 fusion.105
  422.0 13.9 %convolution_bitcast_fusion.4 = f32[4096,1024]{0,1:T(8,128)} fusion(bf16[512,4096]{1,0:T(8,128)(2,1)} %all-gather.7.cloned.1.call-done, f32[512]{0:T(512)S(1)} %get-tuple-element.1859, f32[1024]{0:T(1024)S(1)} %copy-done.17, f32[512,1024]{1,0:T(8,128)} %reshape.537, bf16[512,1024]{1,0:T(8,128)(2,1)} %param.21), kind=kOutput, calls=%fused_computation.168 | convolution fusion | flops 4299685888 | bytes 24123392 | tf_op jit(solution)/shard_map/td,ti->di/dot_general | solution.py:152
  440.6 3.1 copy.152
  443.7 132.6 %all-gather.11.cloned.1.call-done = f32[512,64,128]{2,1,0:T(8,128)} async-done(((f32[16,64,128]{2,1,0:T(8,128)}), f32[512,64,128]{2,1,0:T(8,128)}) %all-gather.11.cloned.1.call-update) | async-done | bytes 16777232 | tf_op jit(solution)/shard_map/all_gather | solution.py:15
  576.3 11.8 %rev.19 = f32[32,16,64,128]{3,2,1,0:T(8,128)} reverse(f32[32,16,64,128]{3,2,1,0:T(8,128)} %bitcast.595), dimensions={0} | reverse | bytes 33554432 | tf_op jit(solution)/shard_map/rev | solution.py:17
  588.1 37.7 %while.111 = (s32[]{:T(128)}, f32[16,64,128]{2,1,0:T(8,128)S(1)}, s32[]{:T(128)}, f32[32,16]{1,0:T(8,128)S(1)}, f32[32,16,64,128]{3,2,1,0:T(8,128)}) while((s32[]{:T(128)}, f32[16,64,128]{2,1,0:T(8,128)S(1)}, s32[]{:T(128)}, f32[32,16]{1,0:T(8,128)S(1)}, f32[32,16,64,128]{3,2,1,0:T(8,128)}) %tuple.234), condition=%wide.region_15.16_spmd.clone.clone, body=%wide.region_14.15_spmd.clone.sunk.clone | while | flops 524292 | bytes 1573145 | solution.py:27
  628.5 163.1 %while.108 = (s32[]{:T(128)}, f32[16,64,128]{2,1,0:T(8,128)S(1)}, bf16[4,128,16,64]{1,3,2,0:T(8,128)(2,1)}, bf16[4,128,1,128]{3,1,2,0:T(8,128)(2,1)}, bf16[4,128...) while((s32[]{:T(128)}, f32[16,64,128]{2,1,0:T(8,128)S(1)}, ...), condition=%wide.region_25.26_spmd.clone.clone, body=%wide.region_16.25_spmd.clone.sunk.clone | while | flops 1263466496 | bytes 32037560 | solution.py:67
  631.4 3.3 fusion.236
  639.1 5.0 fusion.238
  657.4 3.1 fusion.237
  672.2 3.3 fusion.236
  679.8 4.9 fusion.238
  698.1 3.1 fusion.237
  712.9 3.3 fusion.236
  720.5 5.0 fusion.238
  738.8 3.1 fusion.237
  753.6 3.3 fusion.236
  761.2 5.0 fusion.238
  779.5 3.1 fusion.237
  (491 shorter events, 301.5 us)
Async XLA Ops:
  7.2 263.0 %all-gather.9.cloned.1.call-start = ((), (), s32[]{:S(2)}) async-start(), calls=%async_computation.4 | async-start | bytes 17301504 | tf_op jit(solution)/shard_map/all_gather | solution.py:15
  7.9 0.9 copy-start.18
  13.3 0.8 copy-start.6
  13.3 0.8 copy-start.15
  13.3 0.9 copy-start.4
  13.6 2.6 copy-start.8
  20.4 11.8 %copy-start.14 = (s32[16,4]{0,1:T(4,128)S(1)}, s32[16,4]{0,1:T(4,128)}, u32[]{:S(2)}) copy-start(s32[16,4]{0,1:T(4,128)} %param.29) | copy-start | bytes 772
  20.4 382.7 %all-to-all-start = ((bf16[32,128,1024]{2,1,0:T(8,128)(2,1)}), bf16[32,128,1024]{2,1,0:T(8,128)(2,1)}, u32[]{:S(2)}, u32[]{:S(2)}) async-start(bf16[32,128,1024]{2,1,0:T(8,128)(2,1)} %stack.2), calls=%async_computation | async-start | bytes 16777216 | tf_op jit(solution)/shard_map/all_to_all | solution.py:138
  31.4 371.7 %all-gather.7.cloned.1.call-start = ((), (), s32[]{:S(2)}) async-start(), calls=%async_computation.2 | async-start | bytes 5242880 | tf_op jit(solution)/shard_map/all_gather | solution.py:133
  32.2 544.1 %all-gather.11.cloned.1.call-start = ((), (), s32[]{:S(2)}) async-start(), calls=%async_computation.5 | async-start | bytes 17301504 | tf_op jit(solution)/shard_map/all_gather | solution.py:15
  247.0 1.9 copy-start.5
  393.5 4.8 copy-start.1
  398.3 4.9 copy-start.17
  403.2 10.6 %copy-start.2 = (f32[512,1024]{1,0:T(8,128)S(1)}, f32[512,1024]{1,0:T(8,128)}, u32[]{:S(2)}) copy-start(f32[512,1024]{1,0:T(8,128)} %reshape.537) | copy-start | bytes 6291460
  403.2 10.6 %copy-start.3 = (bf16[512,1024]{1,0:T(8,128)(2,1)S(1)}, bf16[512,1024]{1,0:T(8,128)(2,1)}, u32[]{:S(2)}) copy-start(bf16[512,1024]{1,0:T(8,128)(2,1)} %param.21) | copy-start | bytes 3145732
  421.9 379.0 %reduce-scatter.2.cloned.1.call-start = ((), (), s32[]{:S(2)}) async-start(), calls=%async_computation.3 | async-start | bytes 17301504 | tf_op jit(solution)/shard_map/reduce_scatter | solution.py:151
  657.4 6.6 copy-start
  662.5 5.8 copy-start.11
  663.9 4.6 copy-start.9
  698.1 6.5 copy-start
  703.2 5.7 copy-start.11
  704.6 4.6 copy-start.9
  738.8 6.5 copy-start
  743.9 5.7 copy-start.11
  745.3 4.6 copy-start.9
  779.5 6.5 copy-start
  784.7 5.8 copy-start.11
  786.1 4.6 copy-start.9
  795.4 2.3 copy-start.7
  795.4 2.3 copy-start.13
  795.4 2.3 copy-start.16
  795.4 2.3 copy-start.19
  (8 other events, 5.3 us)
Sparse Core Ops, SparseCore 0:
  16.3 253.8 all-gather.8
  271.8 43.7 all-gather.6
  422.0 154.2 all-gather.10
  578.6 222.3 reduce-scatter.1
